TPU v7x, 32 devices: a whole 2x2x4 slice. The times are simulated.
32 devices in a mesh: agent: 8 (over y, x, core), res: 4 (over z).
Axes of the slice: x: 2, y: 2, z: 4, core: 2. Of those that a mesh axis runs over, the one named last changes fastest.
Arguments:
- linear_cost: float32 [2048, 2048], P('agent', 'res'), may hold values from -6 to 6
- agent_type: int32 [2048], P('agent'), may hold values from 0 to 3, as said below
- block_mask: int32 [2048, 16], P('agent', 'res'), may hold values 0 or 1
- inverses: bfloat16 [4, 2048, 2048], P(None, 'res'), as said below
- cost_weight: float32 [2048], P('res'), may hold values from 0.5 to 8
- target: float32 [2048], P('res'), may hold values from -6 to 6
Outputs:
- usage: float32 [2048, 2048], P('agent', 'res')
- shared: float32 [2048], P('res')
- prices: float32 [2048], P('res')
- primal_norm: float32 [5], replicated
- dual_norm: float32 [5], replicated
Inputs may be any that keep to these rules, and one draw needn't show every extreme that they name: Each inverses[k] is exactly symmetric: inverses[k, i, j] equals inverses[k, j, i]. `agent_type`: each aligned block of 256 agents (the agents held by one device along the agent axis) holds exactly 64 agents of each type, in no particular order.
All inputs are finite; a program needn't handle non-finite values. No bound on the sum of `block_mask` on one device may be relied on, other than what follows from the above.
Results may differ from a plain program's by a relative error of at most 0.0039.
Values may be sent and summed in bfloat16 or wider, within the bound.
No kernel may reach another device: no remote copies, remote signals or barrier semaphores. Data moves between devices by JAX's collectives and lax.ppermute only.
A program may use at most 64 MiB of HBM per device.

v0:
```python
import jax
import jax.numpy as jnp
from jax import lax
from jax.sharding import PartitionSpec as P

BLK = 128
ITERS = 5
penalty = 1.0
eps = 1e-06


def on_device(linear_cost, agent_type, block_mask, inverses, cost_weight, target):
    local_agents, local_width = linear_cost.shape
    type_count = inverses.shape[0]
    group_rows = local_agents // type_count
    count = local_agents * lax.axis_size("agent")
    block_count = block_mask.shape[1]
    order = jnp.argsort(agent_type, stable=True)
    restore = jnp.argsort(order, stable=True)
    expand = jnp.broadcast_to(
        block_mask.astype(jnp.float32)[:, :, None], (local_agents, block_count, BLK)
    ).reshape(local_agents, local_width)
    usage = jnp.zeros(linear_cost.shape, jnp.float32)
    mean_usage = jnp.zeros((local_width,), jnp.float32)
    shared = jnp.zeros((local_width,), jnp.float32)
    prices = jnp.zeros((local_width,), jnp.float32)
    primal_list = []
    dual_list = []
    for iteration in range(ITERS):
        rhs = (penalty * (usage - mean_usage + shared - prices) - linear_cost).astype(jnp.bfloat16)
        grouped = rhs[order].reshape(type_count, group_rows, local_width)
        product = jnp.einsum(
            "tas,tws->taw",
            lax.all_gather(grouped, "res", axis=2, tiled=True),
            inverses,
            preferred_element_type=jnp.float32,
        )
        new_usage = product.reshape(local_agents, local_width)[restore]
        new_usage = new_usage * expand
        change_local = penalty * penalty * jnp.sum((new_usage - usage) ** 2)
        usage = new_usage
        column_sum = jnp.sum(usage, axis=0)
        usage_sum = lax.psum(column_sum, "agent")
        dual2 = lax.psum(change_local, ("agent", "res"))
        mean_usage = usage_sum / count
        shared = (cost_weight * target + penalty * (prices + mean_usage)) / (cost_weight + penalty)
        prices = prices + mean_usage - shared
        primal2 = lax.psum(count * jnp.sum((mean_usage - shared) ** 2), "res")
        primal_list.append(jnp.sqrt(primal2 + eps))
        dual_list.append(jnp.sqrt(dual2 + eps))
    primal_norm = jnp.stack(primal_list)
    dual_norm = jnp.stack(dual_list)
    return (usage, shared, prices, primal_norm, dual_norm)


def solution(mesh):
    placed = (
        P("agent", "res"),
        P("agent"),
        P("agent", "res"),
        P(None, "res", None),
        P("res"),
        P("res"),
    )
    return jax.shard_map(
        on_device,
        mesh=mesh,
        in_specs=placed,
        out_specs=(P("agent", "res"), P("res"), P("res"), P(), P()),
        check_vma=False,
    )
```

profile of v0, /device:TPU:12, one launch (start us, length us, event | category | flops | bytes accessed | tf_op | source)
XLA Modules:
  0.0 334.9 jit_solution(6932095263842248031)
XLA Ops:
  7.2 0.0 all-gather.6.cloned.1.call-start
  7.2 3.8 %sort.31 = (s32[256]{0:T(256)}, s32[256]{0:T(256)S(1)}) sort(s32[256]{0:T(256)} %param.7, s32[256]{0:T(256)S(1)} %iota.7), dimensions={0}, to_apply=%region_0.0 | sort | flops 2048 | bytes 4096 | tf_op jit(solution)/shard_map/jit(argsort)/sort | solution.py:18
  11.1 1.1 subtract_convert_fusion.4
  12.2 1.9 gather_fusion
  14.0 0.0 all-gather.6.cloned.1.call-update
  14.0 0.0 all-gather.8.cloned.1.call-start
  14.1 3.2 sort.32
  17.3 0.7 convert_element_type.19
  18.0 0.1 copy.11
  18.1 0.0 copy-start.1
  18.1 0.0 copy-start.3
  18.1 0.0 copy-start
  18.2 25.1 %all-gather.6.cloned.1.call-done = bf16[4,64,2048]{2,1,0:T(8,128)(2,1)} async-done(((bf16[4,64,512]{2,1,0:T(8,128)(2,1)}), bf16[4,64,2048]{2,1,0:T(8,128)(2,1)}) %all-gather.6.cloned.1.call-update) | async-done | bytes 1048592 | tf_op jit(solution)/shard_map/all_gather | solution.py:34
  43.3 6.4 %fusion.13 = f32[4,64,512]{2,1,0:T(8,128)S(1)} fusion(bf16[4,64,2048]{2,1,0:T(8,128)(2,1)} %all-gather.6.cloned.1.call-done, bf16[4,512,2048]{2,1,0:T(8,128)(2,1)} %param.9), kind=kOutput, calls=%fused_computation.56 | convolution fusion | flops 536870912 | bytes 9961472 | tf_op jit(solution)/shard_map/tas,tws->taw/dot_general | solution.py:32
  49.7 1.0 gather_fusion.1
  50.7 0.3 broadcast_in_dim.11
  51.0 0.1 fusion.12
  51.1 11.9 %psum.105 = f32[512]{0:T(512)S(1)} all-reduce(f32[512]{0:T(512)S(1)} %get-tuple-element.44), channel_id=1, replica_groups=mesh['agent'=8,'res'=4] {'agent'}, use_global_device_ids=true, to_apply=%region_3.4 | all-reduce | flops 512 | bytes 4096 | tf_op jit(solution)/shard_map/psum | solution.py:43
  63.0 0.0 copy-done.3
  63.0 0.6 multiply_reduce_fusion.9
  63.6 0.1 subtract_convert_fusion.3
  63.7 1.9 gather_fusion.2
  65.6 0.0 all-gather.8.cloned.1.call-update
  65.6 0.0 all-gather.10.cloned.1.call-start
  65.7 27.5 %all-gather.8.cloned.1.call-done = bf16[4,64,2048]{2,1,0:T(8,128)(2,1)} async-done(((bf16[4,64,512]{2,1,0:T(8,128)(2,1)}), bf16[4,64,2048]{2,1,0:T(8,128)(2,1)}) %all-gather.8.cloned.1.call-update) | async-done | bytes 1048592 | tf_op jit(solution)/shard_map/all_gather | solution.py:34
  93.1 6.4 %fusion.14 = f32[4,64,512]{2,1,0:T(8,128)S(1)} fusion(bf16[4,64,2048]{2,1,0:T(8,128)(2,1)} %all-gather.8.cloned.1.call-done, bf16[4,512,2048]{2,1,0:T(8,128)(2,1)} %param.9), kind=kOutput, calls=%fused_computation.57 | convolution fusion | flops 536870912 | bytes 9961472 | tf_op jit(solution)/shard_map/tas,tws->taw/dot_general | solution.py:32
  99.5 1.0 gather_fusion.3
  100.5 0.1 fusion.11
  100.6 11.9 %psum.106 = f32[512]{0:T(512)S(1)} all-reduce(f32[512]{0:T(512)S(1)} %get-tuple-element.42), channel_id=1, replica_groups=mesh['agent'=8,'res'=4] {'agent'}, use_global_device_ids=true, to_apply=%region_5.6 | all-reduce | flops 512 | bytes 4096 | tf_op jit(solution)/shard_map/psum | solution.py:43
  112.5 0.6 multiply_reduce_fusion.8
  113.1 0.1 subtract_convert_fusion.2
  113.2 1.9 gather_fusion.4
  115.0 0.0 all-gather.10.cloned.1.call-update
  115.1 0.0 all-gather.12.cloned.1.call-start
  115.1 27.5 %all-gather.10.cloned.1.call-done = bf16[4,64,2048]{2,1,0:T(8,128)(2,1)} async-done(((bf16[4,64,512]{2,1,0:T(8,128)(2,1)}), bf16[4,64,2048]{2,1,0:T(8,128)(2,1)}) %all-gather.10.cloned.1.call-update) | async-done | bytes 1048592 | tf_op jit(solution)/shard_map/all_gather | solution.py:34
  142.6 6.4 %fusion.15 = f32[4,64,512]{2,1,0:T(8,128)S(1)} fusion(bf16[4,64,2048]{2,1,0:T(8,128)(2,1)} %all-gather.10.cloned.1.call-done, bf16[4,512,2048]{2,1,0:T(8,128)(2,1)} %param.9), kind=kOutput, calls=%fused_computation.58 | convolution fusion | flops 536870912 | bytes 9961472 | tf_op jit(solution)/shard_map/tas,tws->taw/dot_general | solution.py:32
  148.9 1.0 gather_fusion.5
  149.9 0.1 fusion.10
  150.0 12.1 %psum.107 = f32[512]{0:T(512)S(1)} all-reduce(f32[512]{0:T(512)S(1)} %get-tuple-element.40), channel_id=1, replica_groups=mesh['agent'=8,'res'=4] {'agent'}, use_global_device_ids=true, to_apply=%region_7.8 | all-reduce | flops 512 | bytes 4096 | tf_op jit(solution)/shard_map/psum | solution.py:43
  162.1 0.6 multiply_reduce_fusion.7
  162.7 0.1 subtract_convert_fusion.1
  162.8 1.9 gather_fusion.6
  164.7 0.0 all-gather.12.cloned.1.call-update
  164.7 0.0 all-gather.14.cloned.1.call-start
  164.8 27.4 %all-gather.12.cloned.1.call-done = bf16[4,64,2048]{2,1,0:T(8,128)(2,1)} async-done(((bf16[4,64,512]{2,1,0:T(8,128)(2,1)}), bf16[4,64,2048]{2,1,0:T(8,128)(2,1)}) %all-gather.12.cloned.1.call-update) | async-done | bytes 1048592 | tf_op jit(solution)/shard_map/all_gather | solution.py:34
  192.2 6.4 %fusion.16 = f32[4,64,512]{2,1,0:T(8,128)S(1)} fusion(bf16[4,64,2048]{2,1,0:T(8,128)(2,1)} %all-gather.12.cloned.1.call-done, bf16[4,512,2048]{2,1,0:T(8,128)(2,1)} %param.9), kind=kOutput, calls=%fused_computation.59 | convolution fusion | flops 536870912 | bytes 9961472 | tf_op jit(solution)/shard_map/tas,tws->taw/dot_general | solution.py:32
  198.6 1.8 gather_fusion.7
  200.4 1.2 fusion.9
  201.5 11.9 %psum.108 = f32[512]{0:T(512)S(1)} all-reduce(f32[512]{0:T(512)S(1)} %get-tuple-element.38), channel_id=1, replica_groups=mesh['agent'=8,'res'=4] {'agent'}, use_global_device_ids=true, to_apply=%region_9.10 | all-reduce | flops 512 | bytes 4096 | tf_op jit(solution)/shard_map/psum | solution.py:43
  213.4 0.6 multiply_reduce_fusion.6
  214.0 0.1 subtract_convert_fusion
  214.1 1.9 gather_fusion.8
  216.0 0.0 all-gather.14.cloned.1.call-update
  218.6 24.9 %all-gather.14.cloned.1.call-done = bf16[4,64,2048]{2,1,0:T(8,128)(2,1)} async-done(((bf16[4,64,512]{2,1,0:T(8,128)(2,1)}), bf16[4,64,2048]{2,1,0:T(8,128)(2,1)}) %all-gather.14.cloned.1.call-update) | async-done | bytes 1048592 | tf_op jit(solution)/shard_map/all_gather | solution.py:34
  243.5 6.4 %fusion.17 = f32[4,64,512]{2,1,0:T(8,128)S(1)} fusion(bf16[4,64,2048]{2,1,0:T(8,128)(2,1)} %all-gather.14.cloned.1.call-done, bf16[4,512,2048]{2,1,0:T(8,128)(2,1)} %param.9), kind=kOutput, calls=%fused_computation.60 | convolution fusion | flops 536870912 | bytes 9961472 | tf_op jit(solution)/shard_map/tas,tws->taw/dot_general | solution.py:32
  249.9 1.8 gather_fusion.9
  251.7 2.8 multiply_reduce_fusion
  254.5 11.9 %psum.109 = f32[512]{0:T(512)S(1)} all-reduce(f32[512]{0:T(512)S(1)} %get-tuple-element.14), channel_id=1, replica_groups=mesh['agent'=8,'res'=4] {'agent'}, use_global_device_ids=true, to_apply=%region_11.12 | all-reduce | flops 512 | bytes 4096 | tf_op jit(solution)/shard_map/psum | solution.py:43
  266.3 0.6 multiply_reduce_fusion.5
  267.6 0.6 fusion
  268.2 9.8 %all-reduce.1 = (f32[]{:T(128)}, f32[]{:T(128)}, f32[]{:T(128)}, f32[]{:T(128)}, f32[]{:T(128)}) all-reduce(f32[]{:T(128)S(6)} %mul.99, f32[]{:T(128)S(6)} %mul.100, f32[]{:T(128)S(6)} %mul.101, f32[]{:T(128)S(6)} %mul.102, f32[]{:T(128)S(6)} %mul.103), channel_id=1, replica_groups=mesh['agent'=8,'res'=4] {'res'}, use_global_device_ids=true, to_apply=%region_13.14 | all-reduce | flops 5 | bytes 40 | tf_op jit(solution)/shard_map/psum | solution.py:48
  281.3 42.5 %all-reduce = (f32[]{:T(128)}, f32[]{:T(128)}, f32[]{:T(128)}, f32[]{:T(128)}, f32[]{:T(128)}) all-reduce(f32[]{:T(128)} %get-tuple-element.13, f32[]{:T(128)} %get-tuple-element.12, f32[]{:T(128)} %get-tuple-element.11, f32[]{:T(128)} %get-tuple-element.10, f32[]{:T(128)} %get-tuple-element.9), channel_id=1, replica_groups=mesh['agent'=8,'res'=4] {'agent','res'}, use_global_device_ids=true, to_apply=%region_23.24 | all-reduce | flops 5 | bytes 40 | tf_op jit(solution)/shard_map/psum | solution.py:44
  327.2 0.6 stack.41
  327.8 0.6 stack.47
  (13 shorter events, 0.0 us)
Async XLA Ops:
  7.2 36.1 %all-gather.6.cloned.1.call-start = ((), (), s32[]{:S(2)}) async-start(), calls=%async_computation | async-start | bytes 1310720 | tf_op jit(solution)/shard_map/all_gather | solution.py:34
  14.0 79.1 %all-gather.8.cloned.1.call-start = ((), (), s32[]{:S(2)}) async-start(), calls=%async_computation.1 | async-start | bytes 1310720 | tf_op jit(solution)/shard_map/all_gather | solution.py:34
  18.1 44.9 %copy-start.1 = (f32[512]{0:T(512)S(1)}, f32[512]{0:T(512)}, u32[]{:S(2)}) copy-start(f32[512]{0:T(512)} %param.10) | copy-start | bytes 6148
  18.1 44.9 %copy-start.3 = (f32[512]{0:T(512)S(1)}, f32[512]{0:T(512)}, u32[]{:S(2)}) copy-start(f32[512]{0:T(512)} %param.11) | copy-start | bytes 6148
  18.1 45.5 %copy-start = (f32[256,512]{1,0:T(8,128)S(1)}, f32[256,512]{1,0:T(8,128)}, u32[]{:S(2)}) copy-start(f32[256,512]{1,0:T(8,128)} %param.6) | copy-start | bytes 1572868
  65.6 77.0 %all-gather.10.cloned.1.call-start = ((), (), s32[]{:S(2)}) async-start(), calls=%async_computation.2 | async-start | bytes 1310720 | tf_op jit(solution)/shard_map/all_gather | solution.py:34
  115.1 77.2 %all-gather.12.cloned.1.call-start = ((), (), s32[]{:S(2)}) async-start(), calls=%async_computation.3 | async-start | bytes 1310720 | tf_op jit(solution)/shard_map/all_gather | solution.py:34
  164.7 78.8 %all-gather.14.cloned.1.call-start = ((), (), s32[]{:S(2)}) async-start(), calls=%async_computation.4 | async-start | bytes 1310720 | tf_op jit(solution)/shard_map/all_gather | solution.py:34
  267.0 61.4 %copy-start.2 = (f32[512]{0:T(512)}, f32[512]{0:T(512)S(1)}, u32[]{:S(2)}) copy-start(f32[512]{0:T(512)S(1)} %get-tuple-element.26) | copy-start | bytes 6148
Sparse Core Ops, SparseCore 0:
  14.2 29.0 all-gather.5
  65.7 27.3 all-gather.7
  115.2 27.3 all-gather.9
  164.8 27.3 all-gather.11
  216.1 27.3 all-gather.13
where the time goes:
time: 336 us; the launch traced here: 335 us
  waiting for transfers between devices  132 us (39%)
  blocking collectives  112 us (33%)
  matrix products  31.9 us (9%)
  between operations  23.8 us (7%)
  local copies, waits for them, and re-layouts  17.4 us (5%)
  other arithmetic  17.3 us (5%)
    all_gather x5, waiting for transfers between devices, on_device(): lax.all_gather(grouped, 'res', axis=2, tiled=True)  132 us
    psum x5, blocking collectives, on_device(): usage_sum = lax.psum(column_sum, 'agent')  59.6 us
    psum x1, blocking collectives, on_device(): dual2 = lax.psum(change_local, ('agent', 'res'))  42.5 us
    dot_general x5, matrix products, on_device(): jnp.einsum('tas,tws->taw', lax.all_gather(grouped, 'res', axis=2, tiled=T...  31.9 us
    psum x1, blocking collectives, on_device(): primal2 = lax.psum(count * jnp.sum((mean_usage - shared) ** 2), 'res')  9.78 us
    gather x5, local copies, waits for them, and re-layouts, on_device(): grouped = rhs[order].reshape(type_count, group_rows, local_width)  9.27 us
  transfers between devices with their start and end apart: 5, of which 5 were waited for; matrix products, arithmetic and copies ran while one was open for 1% of the time, Pallas kernels for 0%

commit v1 on v0

--- a/solution.py
+++ b/solution.py
@@ -40,7 +40,10 @@
         change_local = penalty * penalty * jnp.sum((new_usage - usage) ** 2)
         usage = new_usage
         column_sum = jnp.sum(usage, axis=0)
-        usage_sum = lax.psum(column_sum, "agent")
+        devices, usage_sum = (lax.axis_size("agent"), column_sum)
+        for reach in [1 << k for k in range(devices.bit_length() - 1)]:
+            pairs = [(i, i ^ reach) for i in range(devices)]
+            usage_sum = usage_sum + lax.ppermute(usage_sum, "agent", pairs)
         dual2 = lax.psum(change_local, ("agent", "res"))
         mean_usage = usage_sum / count
         shared = (cost_weight * target + penalty * (prices + mean_usage)) / (cost_weight + penalty)

time: 336 us -> 318 us (0.946)
  blocking collectives: 112 us -> 51 us
  waiting for transfers between devices: 132 us -> 163 us
  starting transfers between devices: 0.21 us -> 10.7 us
    psum x5 -> x0, blocking collectives: 59.6 us -> none  [on_device(): usage_sum = lax.psum(column_sum, 'agent')]
    ppermute x0 -> x15, waiting for transfers between devices: none -> 28.5 us  [on_device(): usage_sum = usage_sum + lax.ppermute(usage_sum, 'agent', pairs)]
    ppermute x0 -> x15, starting transfers between devices: none -> 10.4 us  [on_device(): usage_sum = usage_sum + lax.ppermute(usage_sum, 'agent', pairs)]
  transfers between devices with their start and end apart: 5 -> 20, of which waited for: 5 -> 19; matrix products, arithmetic and copies ran while one was open for 1% -> 1% of each run, Pallas kernels for 0% -> 0%
where the time goes in v1:
time: 318 us; the launch traced here: 316 us
  waiting for transfers between devices  163 us (51%)
  blocking collectives  51 us (16%)
  matrix products  31.9 us (10%)
  between operations  24.1 us (8%)
  local copies, waits for them, and re-layouts  17.4 us (5%)
  other arithmetic  17.3 us (5%)
  starting transfers between devices  10.7 us (3%)
    all_gather x5, waiting for transfers between devices, on_device(): lax.all_gather(grouped, 'res', axis=2, tiled=True)  135 us
    psum x1, blocking collectives, on_device(): dual2 = lax.psum(change_local, ('agent', 'res'))  40.7 us
    dot_general x5, matrix products, on_device(): jnp.einsum('tas,tws->taw', lax.all_gather(grouped, 'res', axis=2, tiled=T...  31.9 us
    ppermute x15, waiting for transfers between devices, on_device(): usage_sum = usage_sum + lax.ppermute(usage_sum, 'agent', pairs)  28.5 us
    ppermute x15, starting transfers between devices, on_device(): usage_sum = usage_sum + lax.ppermute(usage_sum, 'agent', pairs)  10.4 us
    psum x1, blocking collectives, on_device(): primal2 = lax.psum(count * jnp.sum((mean_usage - shared) ** 2), 'res')  10.3 us
    gather x5, local copies, waits for them, and re-layouts, on_device(): grouped = rhs[order].reshape(type_count, group_rows, local_width)  9.29 us
    gather x5, local copies, waits for them, and re-layouts, on_device(): new_usage = product.reshape(local_agents, local_width)[restore]  6.45 us
  transfers between devices with their start and end apart: 20, of which 19 were waited for; matrix products, arithmetic and copies ran while one was open for 1% of the time, Pallas kernels for 0%

profile of v1, /device:TPU:12, one launch (start us, length us, event | category | flops | bytes accessed | tf_op | source)
XLA Modules:
  0.0 315.9 jit_solution(9412975653726188234)
XLA Ops:
  7.2 3.8 %sort.31 = (s32[256]{0:T(256)}, s32[256]{0:T(256)S(1)}) sort(s32[256]{0:T(256)} %param.7, s32[256]{0:T(256)S(1)} %iota.7), dimensions={0}, to_apply=%region_0.0 | sort | flops 2048 | bytes 4096 | tf_op jit(solution)/shard_map/jit(argsort)/sort | solution.py:18
  11.1 1.1 subtract_convert_fusion.4
  12.2 1.9 gather_fusion
  14.1 3.2 %sort.32 = (s32[256]{0:T(256)}, s32[256]{0:T(256)S(1)}) sort(s32[256]{0:T(256)S(1)} %get-tuple-element.7, s32[256]{0:T(256)S(1)} %iota.8), dimensions={0}, to_apply=%region_1.2 | sort | flops 2048 | bytes 4096 | tf_op jit(solution)/shard_map/jit(argsort)/sort | solution.py:19
  17.3 0.7 convert_element_type.19
  18.0 0.1 copy.11
  18.2 25.1 %all-gather.6.cloned.1.call-done = bf16[4,64,2048]{2,1,0:T(8,128)(2,1)} async-done(((bf16[4,64,512]{2,1,0:T(8,128)(2,1)}), bf16[4,64,2048]{2,1,0:T(8,128)(2,1)}) %all-gather.6.cloned.1.call-update) | async-done | bytes 1048592 | tf_op jit(solution)/shard_map/all_gather | solution.py:34
  43.3 6.4 %fusion.6 = f32[4,64,512]{2,1,0:T(8,128)S(1)} fusion(bf16[4,64,2048]{2,1,0:T(8,128)(2,1)} %all-gather.6.cloned.1.call-done, bf16[4,512,2048]{2,1,0:T(8,128)(2,1)} %param.9), kind=kOutput, calls=%fused_computation.50 | convolution fusion | flops 536870912 | bytes 9961472 | tf_op jit(solution)/shard_map/tas,tws->taw/dot_general | solution.py:32
  49.7 1.0 gather_fusion.1
  50.7 0.3 broadcast_in_dim.11
  51.2 1.1 collective-permute-done
  52.3 1.5 collective-permute-start.1
  53.8 2.1 collective-permute-done.1
  55.9 0.5 collective-permute-start.2
  56.5 3.0 collective-permute-done.2
  59.5 0.6 multiply_reduce_fusion.9
  60.2 1.9 gather_fusion.2
  62.2 27.5 %all-gather.8.cloned.1.call-done = bf16[4,64,2048]{2,1,0:T(8,128)(2,1)} async-done(((bf16[4,64,512]{2,1,0:T(8,128)(2,1)}), bf16[4,64,2048]{2,1,0:T(8,128)(2,1)}) %all-gather.8.cloned.1.call-update) | async-done | bytes 1048592 | tf_op jit(solution)/shard_map/all_gather | solution.py:34
  89.6 6.4 %fusion.7 = f32[4,64,512]{2,1,0:T(8,128)S(1)} fusion(bf16[4,64,2048]{2,1,0:T(8,128)(2,1)} %all-gather.8.cloned.1.call-done, bf16[4,512,2048]{2,1,0:T(8,128)(2,1)} %param.9), kind=kOutput, calls=%fused_computation.51 | convolution fusion | flops 536870912 | bytes 9961472 | tf_op jit(solution)/shard_map/tas,tws->taw/dot_general | solution.py:32
  96.0 1.0 gather_fusion.3
  97.2 1.1 collective-permute-done.3
  98.3 1.5 collective-permute-start.4
  99.8 2.1 collective-permute-done.4
  101.9 0.6 collective-permute-start.5
  102.5 3.0 collective-permute-done.5
  105.5 0.6 multiply_reduce_fusion.8
  106.1 0.1 subtract_convert_fusion.2
  106.2 1.9 gather_fusion.4
  108.1 0.2 all-gather.12.cloned.1.call-start
  108.4 27.3 %all-gather.10.cloned.1.call-done = bf16[4,64,2048]{2,1,0:T(8,128)(2,1)} async-done(((bf16[4,64,512]{2,1,0:T(8,128)(2,1)}), bf16[4,64,2048]{2,1,0:T(8,128)(2,1)}) %all-gather.10.cloned.1.call-update) | async-done | bytes 1048592 | tf_op jit(solution)/shard_map/all_gather | solution.py:34
  135.6 6.4 %fusion.8 = f32[4,64,512]{2,1,0:T(8,128)S(1)} fusion(bf16[4,64,2048]{2,1,0:T(8,128)(2,1)} %all-gather.10.cloned.1.call-done, bf16[4,512,2048]{2,1,0:T(8,128)(2,1)} %param.9), kind=kOutput, calls=%fused_computation.52 | convolution fusion | flops 536870912 | bytes 9961472 | tf_op jit(solution)/shard_map/tas,tws->taw/dot_general | solution.py:32
  142.0 1.0 gather_fusion.5
  143.2 1.1 collective-permute-done.6
  144.3 1.5 collective-permute-start.7
  145.8 2.1 collective-permute-done.7
  147.9 0.6 collective-permute-start.8
  148.5 3.0 collective-permute-done.8
  151.5 0.6 multiply_reduce_fusion.7
  152.2 1.9 gather_fusion.6
  154.2 27.5 %all-gather.12.cloned.1.call-done = bf16[4,64,2048]{2,1,0:T(8,128)(2,1)} async-done(((bf16[4,64,512]{2,1,0:T(8,128)(2,1)}), bf16[4,64,2048]{2,1,0:T(8,128)(2,1)}) %all-gather.12.cloned.1.call-update) | async-done | bytes 1048592 | tf_op jit(solution)/shard_map/all_gather | solution.py:34
  181.6 6.4 %fusion.9 = f32[4,64,512]{2,1,0:T(8,128)S(1)} fusion(bf16[4,64,2048]{2,1,0:T(8,128)(2,1)} %all-gather.12.cloned.1.call-done, bf16[4,512,2048]{2,1,0:T(8,128)(2,1)} %param.9), kind=kOutput, calls=%fused_computation.53 | convolution fusion | flops 536870912 | bytes 9961472 | tf_op jit(solution)/shard_map/tas,tws->taw/dot_general | solution.py:32
  188.0 1.8 gather_fusion.7
  189.8 1.2 fusion.2
  191.0 1.1 collective-permute-done.9
  192.2 1.5 collective-permute-start.10
  193.6 2.1 collective-permute-done.10
  195.8 0.6 collective-permute-start.11
  196.3 3.0 collective-permute-done.11
  199.3 0.6 multiply_reduce_fusion.6
  200.1 1.9 gather_fusion.8
  202.0 27.5 %all-gather.14.cloned.1.call-done = bf16[4,64,2048]{2,1,0:T(8,128)(2,1)} async-done(((bf16[4,64,512]{2,1,0:T(8,128)(2,1)}), bf16[4,64,2048]{2,1,0:T(8,128)(2,1)}) %all-gather.14.cloned.1.call-update) | async-done | bytes 1048592 | tf_op jit(solution)/shard_map/all_gather | solution.py:34
  229.5 6.4 %fusion.10 = f32[4,64,512]{2,1,0:T(8,128)S(1)} fusion(bf16[4,64,2048]{2,1,0:T(8,128)(2,1)} %all-gather.14.cloned.1.call-done, bf16[4,512,2048]{2,1,0:T(8,128)(2,1)} %param.9), kind=kOutput, calls=%fused_computation.54 | convolution fusion | flops 536870912 | bytes 9961472 | tf_op jit(solution)/shard_map/tas,tws->taw/dot_general | solution.py:32
  235.9 1.8 gather_fusion.9
  237.6 2.8 multiply_reduce_fusion
  240.5 1.2 collective-permute-done.12
  241.6 1.5 collective-permute-start.13
  243.1 2.1 collective-permute-done.13
  245.2 0.5 collective-permute-start.14
  248.4 40.7 %all-reduce = (f32[]{:T(128)}, f32[]{:T(128)}, f32[]{:T(128)}, f32[]{:T(128)}, f32[]{:T(128)}) all-reduce(f32[]{:T(128)} %get-tuple-element.13, f32[]{:T(128)} %get-tuple-element.12, f32[]{:T(128)} %get-tuple-element.11, f32[]{:T(128)} %get-tuple-element.10, f32[]{:T(128)} %get-tuple-element.9), channel_id=1, replica_groups=mesh['agent'=8,'res'=4] {'agent','res'}, use_global_device_ids=true, to_apply=%region_18.19 | all-reduce | flops 5 | bytes 40 | tf_op jit(solution)/shard_map/psum | solution.py:47
  292.6 0.6 multiply_reduce_fusion.5
  293.9 0.6 stack.47
  294.5 10.3 %all-reduce.1 = (f32[]{:T(128)}, f32[]{:T(128)}, f32[]{:T(128)}, f32[]{:T(128)}, f32[]{:T(128)}) all-reduce(f32[]{:T(128)S(6)} %mul.99, f32[]{:T(128)S(6)} %mul.100, f32[]{:T(128)S(6)} %mul.101, f32[]{:T(128)S(6)} %mul.102, f32[]{:T(128)S(6)} %mul.103), channel_id=1, replica_groups=mesh['agent'=8,'res'=4] {'res'}, use_global_device_ids=true, to_apply=%region_8.9 | all-reduce | flops 5 | bytes 40 | tf_op jit(solution)/shard_map/psum | solution.py:51
  308.2 0.6 stack.41
  308.8 0.6 fusion.1
  (52 shorter events, 1.3 us)
Async XLA Ops:
  7.2 36.1 %all-gather.6.cloned.1.call-start = ((), (), s32[]{:S(2)}) async-start(), calls=%async_computation | async-start | bytes 1310720 | tf_op jit(solution)/shard_map/all_gather | solution.py:34
  14.0 75.6 %all-gather.8.cloned.1.call-start = ((), (), s32[]{:S(2)}) async-start(), calls=%async_computation.1 | async-start | bytes 1310720 | tf_op jit(solution)/shard_map/all_gather | solution.py:34
  18.1 41.4 %copy-start.3 = (f32[512]{0:T(512)S(1)}, f32[512]{0:T(512)}, u32[]{:S(2)}) copy-start(f32[512]{0:T(512)} %param.10) | copy-start | bytes 6148
  18.1 41.4 %copy-start.5 = (f32[512]{0:T(512)S(1)}, f32[512]{0:T(512)}, u32[]{:S(2)}) copy-start(f32[512]{0:T(512)} %param.11) | copy-start | bytes 6148
  18.1 42.0 %copy-start = (f32[256,512]{1,0:T(8,128)S(1)}, f32[256,512]{1,0:T(8,128)}, u32[]{:S(2)}) copy-start(f32[256,512]{1,0:T(8,128)} %param.6) | copy-start | bytes 1572868
  51.1 1.2 collective-permute-start
  52.3 3.6 %collective-permute-start.1 = (f32[512]{0:T(512)S(1)}, f32[512]{0:T(512)S(1)}, u32[]{:S(2)}, u32[]{:S(2)}) collective-permute-start(f32[512]{0:T(512)S(1)} %add.181), channel_id=1, source_target_pairs={{0,8},{4,12},{8,0},{12,4},{16,24},{20,28},{24,16},{28,20},{1,9},{5... | collective-permute-start | bytes 6152 | tf_op jit(solution)/shard_map/ppermute | solution.py:46
  55.9 3.6 %collective-permute-start.2 = (f32[512]{0:T(512)S(1)}, f32[512]{0:T(512)S(1)}, u32[]{:S(2)}, u32[]{:S(2)}) collective-permute-start(f32[512]{0:T(512)S(1)} %add.182), channel_id=1, source_target_pairs={{0,16},{4,20},{8,24},{12,28},{16,0},{20,4},{24,8},{28,12},{1,17},{... | collective-permute-start | bytes 6152 | tf_op jit(solution)/shard_map/ppermute | solution.py:46
  62.1 73.5 %all-gather.10.cloned.1.call-start = ((), (), s32[]{:S(2)}) async-start(), calls=%async_computation.2 | async-start | bytes 1310720 | tf_op jit(solution)/shard_map/all_gather | solution.py:34
  97.1 1.2 collective-permute-start.3
  98.3 3.6 %collective-permute-start.4 = (f32[512]{0:T(512)S(1)}, f32[512]{0:T(512)S(1)}, u32[]{:S(2)}, u32[]{:S(2)}) collective-permute-start(f32[512]{0:T(512)S(1)} %add.188), channel_id=1, source_target_pairs={{0,8},{4,12},{8,0},{12,4},{16,24},{20,28},{24,16},{28,20},{1,9},{5... | collective-permute-start | bytes 6152 | tf_op jit(solution)/shard_map/ppermute | solution.py:46
  101.9 3.6 %collective-permute-start.5 = (f32[512]{0:T(512)S(1)}, f32[512]{0:T(512)S(1)}, u32[]{:S(2)}, u32[]{:S(2)}) collective-permute-start(f32[512]{0:T(512)S(1)} %add.189), channel_id=1, source_target_pairs={{0,16},{4,20},{8,24},{12,28},{16,0},{20,4},{24,8},{28,12},{1,17},{... | collective-permute-start | bytes 6152 | tf_op jit(solution)/shard_map/ppermute | solution.py:46
  108.1 73.5 %all-gather.12.cloned.1.call-start = ((), (), s32[]{:S(2)}) async-start(), calls=%async_computation.3 | async-start | bytes 1310720 | tf_op jit(solution)/shard_map/all_gather | solution.py:34
  143.1 1.2 collective-permute-start.6
  144.3 3.6 %collective-permute-start.7 = (f32[512]{0:T(512)S(1)}, f32[512]{0:T(512)S(1)}, u32[]{:S(2)}, u32[]{:S(2)}) collective-permute-start(f32[512]{0:T(512)S(1)} %add.195), channel_id=1, source_target_pairs={{0,8},{4,12},{8,0},{12,4},{16,24},{20,28},{24,16},{28,20},{1,9},{5... | collective-permute-start | bytes 6152 | tf_op jit(solution)/shard_map/ppermute | solution.py:46
  147.9 3.6 %collective-permute-start.8 = (f32[512]{0:T(512)S(1)}, f32[512]{0:T(512)S(1)}, u32[]{:S(2)}, u32[]{:S(2)}) collective-permute-start(f32[512]{0:T(512)S(1)} %add.196), channel_id=1, source_target_pairs={{0,16},{4,20},{8,24},{12,28},{16,0},{20,4},{24,8},{28,12},{1,17},{... | collective-permute-start | bytes 6152 | tf_op jit(solution)/shard_map/ppermute | solution.py:46
  154.1 75.4 %all-gather.14.cloned.1.call-start = ((), (), s32[]{:S(2)}) async-start(), calls=%async_computation.4 | async-start | bytes 1310720 | tf_op jit(solution)/shard_map/all_gather | solution.py:34
  190.9 9.0 %copy-start.1 = (f32[256,512]{1,0:T(8,128)}, f32[256,512]{1,0:T(8,128)S(1)}, u32[]{:S(2)}) copy-start(f32[256,512]{1,0:T(8,128)S(1)} %get-tuple-element.46) | copy-start | bytes 1572868
  190.9 1.2 collective-permute-start.9
  192.2 3.6 %collective-permute-start.10 = (f32[512]{0:T(512)S(1)}, f32[512]{0:T(512)S(1)}, u32[]{:S(2)}, u32[]{:S(2)}) collective-permute-start(f32[512]{0:T(512)S(1)} %add.202), channel_id=1, source_target_pairs={{0,8},{4,12},{8,0},{12,4},{16,24},{20,28},{24,16},{28,20},{1,9},{5... | collective-permute-start | bytes 6152 | tf_op jit(solution)/shard_map/ppermute | solution.py:46
  195.8 3.6 %collective-permute-start.11 = (f32[512]{0:T(512)S(1)}, f32[512]{0:T(512)S(1)}, u32[]{:S(2)}, u32[]{:S(2)}) collective-permute-start(f32[512]{0:T(512)S(1)} %add.203), channel_id=1, source_target_pairs={{0,16},{4,20},{8,24},{12,28},{16,0},{20,4},{24,8},{28,12},{1,17},{... | collective-permute-start | bytes 6152 | tf_op jit(solution)/shard_map/ppermute | solution.py:46
  200.1 37.6 %copy-start.2 = (f32[256,512]{1,0:T(8,128)S(1)}, f32[256,512]{1,0:T(8,128)}, u32[]{:S(2)}) copy-start(f32[256,512]{1,0:T(8,128)} %copy-done.1) | copy-start | bytes 1572868
  240.5 1.2 collective-permute-start.12
  241.6 3.6 %collective-permute-start.13 = (f32[512]{0:T(512)S(1)}, f32[512]{0:T(512)S(1)}, u32[]{:S(2)}, u32[]{:S(2)}) collective-permute-start(f32[512]{0:T(512)S(1)} %add.209), channel_id=1, source_target_pairs={{0,8},{4,12},{8,0},{12,4},{16,24},{20,28},{24,16},{28,20},{1,9},{5... | collective-permute-start | bytes 6152 | tf_op jit(solution)/shard_map/ppermute | solution.py:46
  245.2 47.4 %collective-permute-start.14 = (f32[512]{0:T(512)S(1)}, f32[512]{0:T(512)S(1)}, u32[]{:S(2)}, u32[]{:S(2)}) collective-permute-start(f32[512]{0:T(512)S(1)} %add.210), channel_id=1, source_target_pairs={{0,16},{4,20},{8,24},{12,28},{16,0},{20,4},{24,8},{28,12},{1,17},{... | collective-permute-start | bytes 6152 | tf_op jit(solution)/shard_map/ppermute | solution.py:46
  293.2 16.1 %copy-start.4 = (f32[512]{0:T(512)}, f32[512]{0:T(512)S(1)}, u32[]{:S(2)}) copy-start(f32[512]{0:T(512)S(1)} %get-tuple-element.26) | copy-start | bytes 6148
Sparse Core Ops, SparseCore 0:
  14.2 29.0 all-gather.5
  62.2 27.3 all-gather.7
  108.2 27.3 all-gather.9
  154.2 27.3 all-gather.11
  202.1 27.3 all-gather.13
